TPU v7x, 32 devices: a whole 2x2x4 slice. The times are simulated.
32 devices in a mesh: section: 4 (over x, core), blk: 4 (over z), tp: 2 (over y).
Axes of the slice: x: 2, y: 2, z: 4, core: 2. Of those that a mesh axis runs over, the one named last changes fastest.
Arguments:
- query: bfloat16 [2048, 8192], P(('section', 'blk'), 'tp'), may hold values from -6 to 6
- text_frame: int32 [2048], P(('section', 'blk')), may hold values from 0 to 63
- image_feats: bfloat16 [1024, 8192], P('blk', ('section', 'tp')), may hold values from -6 to 6
- image_frame: int32 [1024], P('blk'), may hold values from 0 to 63, never falling along the last dimension, each value on 1 to 32 neighbouring positions
- kv_weight: bfloat16 [4, 8192, 2, 1024], P('section', None, None, 'tp'), may hold values from -0.0625 to 0.0625
- query_gain: float32 [4, 128], P('section'), may hold values from 0.1 to 1.9
- key_gain: float32 [4, 128], P('section'), may hold values from 0.1 to 1.9
Outputs:
- attended: bfloat16 [2048, 8192], P(('section', 'blk'), 'tp')
Inputs may be any that keep to these rules, and one draw needn't show every extreme that they name: `image_frame`: image frame ids never fall along the image tokens; every frame has at least one token.
All inputs are finite; a program needn't handle non-finite values.
Results may differ from a plain program's by a relative error of at most 0.007.
Values may be sent and summed in bfloat16 or wider, within the bound.
A program may use at most 128 MiB of HBM per device.

v0:
```python
import jax
import jax.numpy as jnp
from jax import lax
from jax.sharding import PartitionSpec as P


def normalize(x):
    return x * lax.rsqrt(jnp.mean(x * x, axis=-1, keepdims=True) + 1e-05)


def per_device(query, text_frame, image_feats, image_frame, kv_weight, query_gain, key_gain):
    head_size = query_gain.shape[1]
    feat_width = kv_weight.shape[1]
    kv_cols = kv_weight.shape[3]
    heads_kv = kv_cols // head_size
    text_rows = query.shape[0]
    groups = query.shape[1] // kv_cols
    block_rows = image_feats.shape[0]
    weight_flat = kv_weight[0].reshape(feat_width, 2 * kv_cols)
    wide = lax.all_gather(image_feats, ("section", "tp"), axis=1, tiled=True)
    proj = jnp.dot(wide, weight_flat, preferred_element_type=jnp.float32)
    proj = proj.reshape(block_rows, 2, heads_kv, head_size)
    keys = (normalize(proj[:, 0]) * key_gain[0]).astype(jnp.bfloat16)
    values = proj[:, 1].astype(jnp.bfloat16)
    key_value = jnp.stack([keys, values], axis=1).reshape(block_rows, 2, kv_cols)
    qrows = query.astype(jnp.float32).reshape(text_rows, heads_kv, groups, head_size)
    qn = (normalize(qrows) * query_gain[0] * head_size ** (-0.5)).astype(jnp.bfloat16)
    block = lax.all_gather(key_value, "blk", axis=0, tiled=True)
    frames = lax.all_gather(image_frame, "blk", axis=0, tiled=True)
    count = block.shape[0]
    keys_part = block[:, 0].reshape(count, heads_kv, head_size)
    values_part = block[:, 1].reshape(count, heads_kv, head_size)
    scores = jnp.einsum("tkgd,skd->kgts", qn, keys_part, preferred_element_type=jnp.float32)
    allowed = frames[None, :] <= text_frame[:, None]
    weights = jnp.where(allowed, jnp.exp(scores), jnp.float32(0.0))
    total = jnp.sum(weights, axis=-1)
    wb = weights.astype(jnp.bfloat16)
    summed = jnp.einsum("kgts,skd->kgtd", wb, values_part, preferred_element_type=jnp.float32)
    result = summed / total[..., None]
    return (
        result.transpose(2, 0, 1, 3)
        .reshape(text_rows, heads_kv * groups * head_size)
        .astype(jnp.bfloat16)
    )


def solution(mesh):
    return jax.shard_map(
        per_device,
        mesh=mesh,
        in_specs=(
            P(("section", "blk"), "tp"),
            P(("section", "blk")),
            P("blk", ("section", "tp")),
            P("blk"),
            P("section", None, None, "tp"),
            P("section", None),
            P("section", None),
        ),
        out_specs=P(("section", "blk"), "tp"),
        check_vma=False,
    )
```

profile of v0, /device:TPU:0, one launch (start us, length us, event | category | flops | bytes accessed | tf_op | source)
XLA Modules:
  0.0 122.1 jit_solution(2899087948636825844)
XLA Ops:
  6.5 0.7 all-gather.4.cloned.1.call-update
  7.3 0.0 all-gather.6.cloned.1.call-start
  7.3 16.7 %copy.35 = bf16[1024,8,2,512]{3,1,2,0:T(8,128)(2,1)} copy(bf16[1024,8,2,512]{3,2,1,0:T(2,128)(2,1)} %bitcast.52) | data formatting | bytes 33554432
  24.0 21.3 %copy.22 = bf16[1024,8192]{1,0:T(8,128)(2,1)} copy(bf16[1024,8192]{0,1:T(8,128)(2,1)} %bitcast.49) | data formatting | bytes 33554432 | tf_op jit(solution)/shard_map/dot_general | solution.py:21
  45.3 3.4 %all-gather.4.cloned.1.call-done = bf16[256,8192]{1,0:T(8,128)(2,1)} async-done(((bf16[256,1024]{1,0:T(8,128)(2,1)}), bf16[256,8192]{1,0:T(8,128)(2,1)}) %all-gather.4.cloned.1.call-update) | async-done | bytes 4194320 | tf_op jit(solution)/shard_map/all_gather | solution.py:20
  48.7 9.4 %fusion.6 = f32[256,2,4,128]{0,3,2,1:T(8,128)S(1)} fusion(bf16[2,4,128,8192]{3,2,1,0:T(8,128)(2,1)} %bitcast.53, bf16[256,8192]{1,0:T(8,128)(2,1)} %all-gather.4.cloned.1.call-done), kind=kOutput, calls=%fused_computation.6 | convolution fusion | flops 4294967296 | bytes 22020096 | tf_op jit(solution)/shard_map/dot_general | solution.py:21
  58.2 0.1 multiply_reduce_fusion.1
  58.3 0.1 multiply_convert_fusion.1
  58.4 0.8 pad_maximum_fusion
  59.2 0.0 all-gather.6.cloned.1.call-update
  59.2 0.2 convert_bitcast_fusion
  59.5 0.0 copy-start.1
  59.5 0.4 copy.36
  59.9 0.8 multiply_reduce_fusion
  60.7 0.1 copy.23
  60.8 0.2 copy.24
  61.0 11.0 %all-gather = s32[4,1,256]{2,1,0:T(1,128)S(1)} all-gather(s32[1,1,256]{2,1,0:T(1,128)S(1)} %bitcast.61), channel_id=1, replica_groups=mesh['section'=4,'blk'=4,'tp'=2] {'blk'}, dimensions={0}, use_global_device_ids=true | all-gather | bytes 5120 | tf_op jit(solution)/shard_map/all_gather | solution.py:29
  72.0 0.2 broadcast_compare_fusion
  72.2 0.7 multiply_convert_fusion
  73.0 32.7 %all-gather.6.cloned.1.call-done = bf16[1024,2,512]{0,2,1:T(8,128)(2,1)} async-done(((bf16[256,2,512]{0,2,1:T(8,128)(2,1)}), bf16[1024,2,512]{0,2,1:T(8,128)(2,1)}) %all-gather.6.cloned.1.call-update) | async-done | bytes 2097168 | tf_op jit(solution)/shard_map/all_gather | solution.py:28
  105.6 1.7 %fusion.14 = (bf16[1024,1,512]{0,2,1:T(8,128)(2,1)S(1)}, bf16[1024,1,512]{0,2,1:T(8,128)(2,1)S(1)}) fusion(bf16[1024,2,512]{0,2,1:T(8,128)(2,1)} %all-gather.6.cloned.1.call-done), kind=kLoop, calls=%fused_computation.23 | loop fusion | bytes 4194304 | tf_op jit(solution)/shard_map/slice | solution.py:31
  107.4 3.4 %fusion = (f32[4,8,128]{2,1,0:T(8,128)S(1)}, f32[4,1024,128,8]{2,1,3,0:T(8,128)S(1)}) fusion(pred[128,1024]{0,1:T(8,128)(4,1)S(1)} %broadcast_compare_fusion, bf16[1024,4,128,1]{0,2,3,1:T(8,128)(2,1)S(1)} %bitcast.54, bf16[128,4,8,128]{3,2,1,0:T(8,128)(2,1)S(1)} %multiply_convert_fusion), kind=kOutput, calls=%fused_computation.1 | convolution fusion | flops 1082126336 | bytes 19021824 | tf_op jit(solution)/shard_map/tkgd,skd->kgts/dot_general | solution.py:33
  110.8 3.2 %fusion.8 = bf16[128,4,8,128]{0,3,2,1:T(8,128)(2,1)S(1)} fusion(bf16[1024,4,128,1]{0,2,3,1:T(8,128)(2,1)S(1)} %bitcast.57, f32[4,1024,128,8]{2,1,3,0:T(8,128)S(1)} %get-tuple-element.8, pred[128,1024]{0,1:T(8,128)(4,1)S(1)} %broadcast_compare_fusion, f32[128,4,8]{0,2,1:T(8,128)S(1)} %bitcast.60), kind=kOutput, calls=%fused_computation.9 | convolution fusion | flops 1083179008 | bytes 19021824 | tf_op jit(solution)/shard_map/kgts,skd->kgtd/dot_general | solution.py:38
  114.0 1.3 %copy.28 = bf16[128,4096]{1,0:T(8,128)(2,1)} copy(bf16[128,4096]{0,1:T(8,128)(2,1)S(1)} %bitcast.55) | data formatting | bytes 2097152 | tf_op jit(solution)/shard_map/convert_element_type | solution.py:43
  (13 shorter events, 0.1 us)
Async XLA Ops:
  6.5 42.2 %all-gather.4.cloned.1.call-start = ((), (), s32[]{:S(2)}) async-start(), calls=%async_computation | async-start | bytes 4718592 | tf_op jit(solution)/shard_map/all_gather | solution.py:20
  7.3 98.4 %all-gather.6.cloned.1.call-start = ((), (), s32[]{:S(2)}) async-start(), calls=%async_computation.1 | async-start | bytes 2621440 | tf_op jit(solution)/shard_map/all_gather | solution.py:28
  48.7 9.6 %copy-start.4 = (f32[1,128]{1,0:T(1,128)S(1)}, f32[1,128]{1,0:T(1,128)}, u32[]{:S(2)}) copy-start(f32[1,128]{1,0:T(1,128)} %param.13) | copy-start | bytes 1540
  48.7 10.5 %copy-start = (bf16[128,4096]{1,0:T(8,128)(2,1)S(1)}, bf16[128,4096]{1,0:T(8,128)(2,1)}, u32[]{:S(2)}) copy-start(bf16[128,4096]{1,0:T(8,128)(2,1)} %param.7) | copy-start | bytes 3145732
  59.5 1.5 %copy-start.1 = (s32[256]{0:T(256)S(1)}, s32[256]{0:T(256)}, u32[]{:S(2)}) copy-start(s32[256]{0:T(256)} %param.10) | copy-start | bytes 3076
  59.5 12.5 %copy-start.2 = (s32[128]{0:T(128)S(1)}, s32[128]{0:T(128)}, u32[]{:S(2)}) copy-start(s32[128]{0:T(128)} %param.8) | copy-start | bytes 1540
  59.5 12.7 %copy-start.3 = (f32[1,128]{1,0:T(1,128)S(1)}, f32[1,128]{1,0:T(1,128)}, u32[]{:S(2)}) copy-start(f32[1,128]{1,0:T(1,128)} %param.12) | copy-start | bytes 1540
Sparse Core Ops, SparseCore 0:
  9.3 39.4 all-gather.3
  59.4 46.2 all-gather.5
where the time goes:
time: 123 us; the launch traced here: 122 us
  local copies, waits for them, and re-layouts  41.7 us (34%)
  waiting for transfers between devices  36.8 us (30%)
  matrix products  16 us (13%)
  between operations  13.6 us (11%)
  blocking collectives  11 us (9%)
  other arithmetic  2.98 us (2%)
    all_gather x1, waiting for transfers between devices, per_device(): block = lax.all_gather(key_value, 'blk', axis=0, tiled=True)  32.7 us
    dot_general x1, local copies, waits for them, and re-layouts, per_device(): proj = jnp.dot(wide, weight_flat, preferred_element_type=jnp.float32)  21.3 us
    unnamed x12, local copies, waits for them, and re-layouts  17.1 us
    all_gather x1, blocking collectives, per_device(): frames = lax.all_gather(image_frame, 'blk', axis=0, tiled=True)  11 us
    dot_general x1, matrix products, per_device(): proj = jnp.dot(wide, weight_flat, preferred_element_type=jnp.float32)  9.44 us
    dot_general x1, matrix products, per_device(): jnp.einsum('tkgd,skd->kgts', qn, keys_part, preferred_element_type=jnp.fl...  3.4 us
    all_gather x1, waiting for transfers between devices, per_device(): wide = lax.all_gather(image_feats, ('section', 'tp'), axis=1, tiled=True)  3.39 us
    dot_general x1, matrix products, per_device(): jnp.einsum('kgts,skd->kgtd', wb, values_part, preferred_element_type=jnp....  3.22 us
  transfers between devices with their start and end apart: 2, of which 2 were waited for; matrix products, arithmetic and copies ran while one was open for 33% of the time, Pallas kernels for 0%

commit v1 on v0

--- a/solution.py
+++ b/solution.py
@@ -26,7 +26,12 @@
     qrows = query.astype(jnp.float32).reshape(text_rows, heads_kv, groups, head_size)
     qn = (normalize(qrows) * query_gain[0] * head_size ** (-0.5)).astype(jnp.bfloat16)
     block = lax.all_gather(key_value, "blk", axis=0, tiled=True)
-    frames = lax.all_gather(image_frame, "blk", axis=0, tiled=True)
+    ring = [image_frame]
+    for hop in range(3):
+        ring.append(lax.ppermute(ring[-1], "blk", [(dev, (dev + 1) % 4) for dev in range(4)]))
+    frames = jnp.roll(
+        jnp.concatenate(ring[::-1], axis=0), (lax.axis_index("blk") + 1) * ring[0].shape[0], axis=0
+    )
     count = block.shape[0]
     keys_part = block[:, 0].reshape(count, heads_kv, head_size)
     values_part = block[:, 1].reshape(count, heads_kv, head_size)

time: 123 us -> 123 us (level)
  blocking collectives: 11 us -> 0 us
  waiting for transfers between devices: 36.8 us -> 46.3 us
  starting transfers between devices: 0.04 us -> 1.58 us
    ppermute x0 -> x3, waiting for transfers between devices: none -> 12.2 us  [per_device(): lax.ppermute(ring[-1], 'blk', [(dev, (dev + 1) % 4) for dev in range(4)])]
    all_gather x1 -> x0, blocking collectives: 11 us -> none  [per_device(): frames = lax.all_gather(image_frame, 'blk', axis=0, tiled=True)]
    all_gather x1, waiting for transfers between devices: 32.7 us -> 29.8 us  [per_device(): block = lax.all_gather(key_value, 'blk', axis=0, tiled=True)]
    ppermute x0 -> x3, starting transfers between devices: none -> 1.54 us  [per_device(): lax.ppermute(ring[-1], 'blk', [(dev, (dev + 1) % 4) for dev in range(4)])]
    unnamed x12 -> x19, local copies, waits for them, and re-layouts: 17.1 us -> 17.1 us
  transfers between devices with their start and end apart: 2 -> 5, of which waited for: 2 -> 5; matrix products, arithmetic and copies ran while one was open for 33% -> 33% of each run, Pallas kernels for 0% -> 0%
where the time goes in v1:
time: 123 us; the launch traced here: 122 us
  waiting for transfers between devices  46.3 us (38%)
  local copies, waits for them, and re-layouts  41.7 us (34%)
  matrix products  16.2 us (13%)
  between operations  13.6 us (11%)
  other arithmetic  2.94 us (2%)
  starting transfers between devices  1.58 us (1%)
    all_gather x1, waiting for transfers between devices, per_device(): block = lax.all_gather(key_value, 'blk', axis=0, tiled=True)  29.8 us
    dot_general x1, local copies, waits for them, and re-layouts, per_device(): proj = jnp.dot(wide, weight_flat, preferred_element_type=jnp.float32)  21.2 us
    unnamed x19, local copies, waits for them, and re-layouts  17.1 us
    ppermute x3, waiting for transfers between devices, per_device(): lax.ppermute(ring[-1], 'blk', [(dev, (dev + 1) % 4) for dev in range(4)])  12.2 us
    dot_general x1, matrix products, per_device(): proj = jnp.dot(wide, weight_flat, preferred_element_type=jnp.float32)  9.44 us
    all_gather x1, waiting for transfers between devices, per_device(): wide = lax.all_gather(image_feats, ('section', 'tp'), axis=1, tiled=True)  3.52 us
    dot_general x1, matrix products, per_device(): jnp.einsum('tkgd,skd->kgts', qn, keys_part, preferred_element_type=jnp.fl...  3.48 us
    dot_general x1, matrix products, per_device(): jnp.einsum('kgts,skd->kgtd', wb, values_part, preferred_element_type=jnp....  3.29 us
  transfers between devices with their start and end apart: 5, of which 5 were waited for; matrix products, arithmetic and copies ran while one was open for 33% of the time, Pallas kernels for 0%

profile of v1, /device:TPU:0, one launch (start us, length us, event | category | flops | bytes accessed | tf_op | source)
XLA Modules:
  0.0 122.3 jit_solution(9378162278102118457)
XLA Ops:
  6.5 0.7 all-gather.3.cloned.1.call-update
  7.3 16.7 %copy.35 = bf16[1024,8,2,512]{3,1,2,0:T(8,128)(2,1)} copy(bf16[1024,8,2,512]{3,2,1,0:T(2,128)(2,1)} %bitcast.50) | data formatting | bytes 33554432
  24.0 21.2 %copy.22 = bf16[1024,8192]{1,0:T(8,128)(2,1)} copy(bf16[1024,8192]{0,1:T(8,128)(2,1)} %bitcast.47) | data formatting | bytes 33554432 | tf_op jit(solution)/shard_map/dot_general | solution.py:21
  45.2 3.5 %all-gather.3.cloned.1.call-done = bf16[256,8192]{1,0:T(8,128)(2,1)} async-done(((bf16[256,1024]{1,0:T(8,128)(2,1)}), bf16[256,8192]{1,0:T(8,128)(2,1)}) %all-gather.3.cloned.1.call-update) | async-done | bytes 4194320 | tf_op jit(solution)/shard_map/all_gather | solution.py:20
  48.7 9.4 %fusion.6 = f32[256,2,4,128]{0,3,2,1:T(8,128)S(1)} fusion(bf16[2,4,128,8192]{3,2,1,0:T(8,128)(2,1)} %bitcast.51, bf16[256,8192]{1,0:T(8,128)(2,1)} %all-gather.3.cloned.1.call-done), kind=kOutput, calls=%fused_computation.6 | convolution fusion | flops 4294967296 | bytes 22020096 | tf_op jit(solution)/shard_map/dot_general | solution.py:21
  58.3 0.1 multiply_convert_fusion.1
  58.4 0.8 pad_maximum_fusion
  59.3 1.5 %collective-permute-start = (s32[256]{0:T(256)S(1)}, s32[256]{0:T(256)S(1)}, u32[]{:S(2)}, u32[]{:S(2)}) collective-permute-start(s32[256]{0:T(256)S(1)} %copy-done.1), channel_id=1, source_target_pairs={{0,2},{2,4},{4,6},{6,0},{1,3},{3,5},{5,7},{7,1},{8,10},{10,12},{12... | collective-permute-start | bytes 3080 | tf_op jit(solution)/shard_map/ppermute | solution.py:31
  60.8 0.2 convert_bitcast_fusion
  61.0 0.4 copy.36
  61.4 0.8 multiply_reduce_fusion
  62.2 0.1 copy.23
  62.3 0.2 copy.24
  62.5 2.2 %collective-permute-done = s32[256]{0:T(256)S(1)} collective-permute-done((s32[256]{0:T(256)S(1)}, s32[256]{0:T(256)S(1)}, u32[]{:S(2)}, u32[]{:S(2)}) %collective-permute-start) | collective-permute-done | bytes 1056 | tf_op jit(solution)/shard_map/ppermute | solution.py:31
  64.7 0.7 multiply_convert_fusion
  65.4 4.6 %collective-permute-done.1 = s32[256]{0:T(256)S(1)} collective-permute-done((s32[256]{0:T(256)S(1)}, s32[256]{0:T(256)S(1)}, u32[]{:S(2)}, u32[]{:S(2)}) %collective-permute-start.1) | collective-permute-done | bytes 1056 | tf_op jit(solution)/shard_map/ppermute | solution.py:31
  70.0 5.4 %collective-permute-done.2 = s32[256]{0:T(256)S(1)} collective-permute-done((s32[256]{0:T(256)S(1)}, s32[256]{0:T(256)S(1)}, u32[]{:S(2)}, u32[]{:S(2)}) %collective-permute-start.2) | collective-permute-done | bytes 1056 | tf_op jit(solution)/shard_map/ppermute | solution.py:31
  75.6 0.1 dynamic_slice.4
  75.7 0.2 broadcast_compare_fusion
  75.9 29.8 %all-gather.5.cloned.1.call-done = bf16[1024,2,512]{0,2,1:T(8,128)(2,1)} async-done(((bf16[256,2,512]{0,2,1:T(8,128)(2,1)}), bf16[1024,2,512]{0,2,1:T(8,128)(2,1)}) %all-gather.5.cloned.1.call-update) | async-done | bytes 2097168 | tf_op jit(solution)/shard_map/all_gather | solution.py:28
  105.7 1.7 %fusion.14 = (bf16[1024,1,512]{0,2,1:T(8,128)(2,1)S(1)}, bf16[1024,1,512]{0,2,1:T(8,128)(2,1)S(1)}) fusion(bf16[1024,2,512]{0,2,1:T(8,128)(2,1)} %all-gather.5.cloned.1.call-done), kind=kLoop, calls=%fused_computation.31 | loop fusion | bytes 4194304 | tf_op jit(solution)/shard_map/slice | solution.py:36
  107.4 3.5 %fusion = (f32[4,8,128]{2,1,0:T(8,128)S(1)}, f32[4,1024,128,8]{2,1,3,0:T(8,128)S(1)}) fusion(pred[128,1024]{0,1:T(8,128)(4,1)S(1)} %broadcast_compare_fusion, bf16[1024,4,128,1]{0,2,3,1:T(8,128)(2,1)S(1)} %bitcast.52, bf16[128,4,8,128]{3,2,1,0:T(8,128)(2,1)S(1)} %multiply_convert_fusion), kind=kOutput, calls=%fused_computation.1 | convolution fusion | flops 1082126336 | bytes 19021824 | tf_op jit(solution)/shard_map/tkgd,skd->kgts/dot_general | solution.py:38
  110.9 3.3 %fusion.8 = bf16[128,4,8,128]{0,3,2,1:T(8,128)(2,1)S(1)} fusion(bf16[1024,4,128,1]{0,2,3,1:T(8,128)(2,1)S(1)} %bitcast.55, f32[4,1024,128,8]{2,1,3,0:T(8,128)S(1)} %get-tuple-element.8, pred[128,1024]{0,1:T(8,128)(4,1)S(1)} %broadcast_compare_fusion, f32[128,4,8]{0,2,1:T(8,128)S(1)} %bitcast.57), kind=kOutput, calls=%fused_computation.9 | convolution fusion | flops 1083179008 | bytes 19021824 | tf_op jit(solution)/shard_map/kgts,skd->kgtd/dot_general | solution.py:43
  114.2 1.3 %copy.28 = bf16[128,4096]{1,0:T(8,128)(2,1)} copy(bf16[128,4096]{0,1:T(8,128)(2,1)S(1)} %bitcast.53) | data formatting | bytes 2097152 | tf_op jit(solution)/shard_map/convert_element_type | solution.py:48
  (28 shorter events, 0.2 us)
Async XLA Ops:
  6.5 42.2 %all-gather.3.cloned.1.call-start = ((), (), s32[]{:S(2)}) async-start(), calls=%async_computation | async-start | bytes 4718592 | tf_op jit(solution)/shard_map/all_gather | solution.py:20
  7.3 98.4 %all-gather.5.cloned.1.call-start = ((), (), s32[]{:S(2)}) async-start(), calls=%async_computation.1 | async-start | bytes 2621440 | tf_op jit(solution)/shard_map/all_gather | solution.py:28
  48.7 9.6 %copy-start.4 = (f32[1,128]{1,0:T(1,128)S(1)}, f32[1,128]{1,0:T(1,128)}, u32[]{:S(2)}) copy-start(f32[1,128]{1,0:T(1,128)} %param.13) | copy-start | bytes 1540
  48.7 10.5 %copy-start.1 = (s32[256]{0:T(256)S(1)}, s32[256]{0:T(256)}, u32[]{:S(2)}) copy-start(s32[256]{0:T(256)} %param.10) | copy-start | bytes 3076
  48.7 12.1 %copy-start = (bf16[128,4096]{1,0:T(8,128)(2,1)S(1)}, bf16[128,4096]{1,0:T(8,128)(2,1)}, u32[]{:S(2)}) copy-start(bf16[128,4096]{1,0:T(8,128)(2,1)} %param.7) | copy-start | bytes 3145732
  59.3 5.4 %collective-permute-start = (s32[256]{0:T(256)S(1)}, s32[256]{0:T(256)S(1)}, u32[]{:S(2)}, u32[]{:S(2)}) collective-permute-start(s32[256]{0:T(256)S(1)} %copy-done.1), channel_id=1, source_target_pairs={{0,2},{2,4},{4,6},{6,0},{1,3},{3,5},{5,7},{7,1},{8,10},{10,12},{12... | collective-permute-start | bytes 3080 | tf_op jit(solution)/shard_map/ppermute | solution.py:31
  61.0 3.7 %copy-start.2 = (f32[1,128]{1,0:T(1,128)S(1)}, f32[1,128]{1,0:T(1,128)}, u32[]{:S(2)}) copy-start(f32[1,128]{1,0:T(1,128)} %param.12) | copy-start | bytes 1540
  61.4 14.3 %copy-start.3 = (s32[128]{0:T(128)S(1)}, s32[128]{0:T(128)}, u32[]{:S(2)}) copy-start(s32[128]{0:T(128)} %param.8) | copy-start | bytes 1540
  64.7 5.4 %collective-permute-start.1 = (s32[256]{0:T(256)S(1)}, s32[256]{0:T(256)S(1)}, u32[]{:S(2)}, u32[]{:S(2)}) collective-permute-start(s32[256]{0:T(256)S(1)} %collective-permute-done), channel_id=1, source_target_pairs={{0,2},{2,4},{4,6},{6,0},{1,3},{3,5},{5,7},{7,1},{8,10},{10,12},{12... | collective-permute-start | bytes 3080 | tf_op jit(solution)/shard_map/ppermute | solution.py:31
  70.0 5.4 %collective-permute-start.2 = (s32[256]{0:T(256)S(1)}, s32[256]{0:T(256)S(1)}, u32[]{:S(2)}, u32[]{:S(2)}) collective-permute-start(s32[256]{0:T(256)S(1)} %collective-permute-done.1), channel_id=1, source_target_pairs={{0,2},{2,4},{4,6},{6,0},{1,3},{3,5},{5,7},{7,1},{8,10},{10,12},{12... | collective-permute-start | bytes 3080 | tf_op jit(solution)/shard_map/ppermute | solution.py:31
Sparse Core Ops, SparseCore 0:
  9.3 39.4 all-gather.2
  59.4 46.2 all-gather.4
